TPU v7x, 32 devices: a whole 2x2x4 slice. The times are simulated.
32 devices in a mesh: dp: 2 (over y), pipe: 4 (over x, core), seq: 4 (over z).
Axes of the slice: x: 2, y: 2, z: 4, core: 2. Of those that a mesh axis runs over, the one named last changes fastest.
Arguments:
- query_states: bfloat16 [8, 512, 8192], P(('dp', 'pipe'), 'seq'), parts along dimension 0, may hold values from -15 to 15
- projected_keys: bfloat16 [8, 512, 1024], P(('dp', 'pipe'), 'seq'), parts along dimension 0, may hold values from -8 to 8
- projected_values: bfloat16 [8, 512, 1024], P(('dp', 'pipe'), 'seq'), parts along dimension 0, may hold values from -6 to 6
- positions: int32 [8, 512], P(('dp', 'pipe'), 'seq'), parts along dimension 0, may hold values from 0 to 1023, as said below
- segments: int32 [8, 512], P(('dp', 'pipe'), 'seq'), parts along dimension 0, may hold values from 0 to 3, as said below
Outputs:
- handed: bfloat16 [8, 512, 8192], P(('dp', 'pipe'), 'seq'), parts along dimension 0
There are 2 independent parts, one for each index of `dp`. A program takes and returns all parts, laid end to end along the dimension named above; each array names one. Nothing has to cross between parts.
Inputs may be any that keep to these rules, and one draw needn't show every extreme that they name: `segments`: within each micro-batch ids never fall along the sequence, start at 0, every id occurs, and every document holds 4 or more tokens. `positions`: within a document a position is one more than the previous token's; the first document of each micro-batch starts at 0, and the last token of each micro-batch has position 1023.
All inputs are finite; a program needn't handle non-finite values.
Results may differ from a plain program's by a relative error of at most 0.0014.
The roundings to bfloat16 on the way count: a program that leaves them out, or rounds other values in their place, can miss the bound.
Values may be sent and summed in bfloat16 or wider, within the bound.
No kernel may reach another device: no remote copies, remote signals or barrier semaphores. Data moves between devices by JAX's collectives and lax.ppermute only.
A program may use at most 64 MiB of HBM per device.

v0:
```python
import math

import jax
import jax.numpy as jnp
from jax import lax
from jax.sharding import PartitionSpec as P

QUERY_HEADS = 64
KEY_VALUE_HEADS = 8
HEAD_SIZE = 128


rope_theta = 1000000.0
yarn_factor = 4.0
trained_length = 32768.0
fast_beta = 32.0
slow_beta = 1.0
masked_score = -1e30


def passed_along(block, axis, distance):
    devices = range(lax.axis_size(axis))
    route = [((i - distance) % len(devices), i) for i in devices]
    return lax.ppermute(block, axis, route)


def yarn_tables(positions, head_dim):
    half_dim = head_dim // 2
    pair_index = jnp.arange(half_dim, dtype=jnp.float32)
    base_freq = 1.0 / rope_theta ** (2.0 * pair_index / head_dim)
    lower = math.floor(
        head_dim
        * math.log(trained_length / (fast_beta * 2.0 * math.pi))
        / (2.0 * math.log(rope_theta))
    )
    upper = math.ceil(
        head_dim
        * math.log(trained_length / (slow_beta * 2.0 * math.pi))
        / (2.0 * math.log(rope_theta))
    )
    lower = max(lower, 0)
    upper = min(upper, head_dim - 1)
    upper = max(upper, lower + 1)
    ramp_value = jnp.clip((pair_index - lower) / (upper - lower), 0.0, 1.0)
    keep_share = 1.0 - ramp_value
    inv_freq = base_freq / yarn_factor * (1.0 - keep_share) + base_freq * keep_share
    attn_gain = 0.1 * math.log(yarn_factor) + 1.0
    angles = positions.astype(jnp.float32)[..., None] * inv_freq
    return (jnp.cos(angles) * attn_gain, jnp.sin(angles) * attn_gain)


def apply_rotation(states, cosine_table, sine_table):
    half_dim = states.shape[-1] // 2
    first_half = states[..., :half_dim]
    second_half = states[..., half_dim:]
    return jnp.concatenate(
        [
            first_half * cosine_table - second_half * sine_table,
            second_half * cosine_table + first_half * sine_table,
        ],
        axis=-1,
    )


def empty_running(query_rows, kv_count, group_count):
    return (
        jnp.full((query_rows, kv_count, group_count), masked_score, jnp.float32),
        jnp.zeros((query_rows, kv_count, group_count), jnp.float32),
        jnp.zeros((query_rows, kv_count, group_count, HEAD_SIZE), jnp.float32),
    )


def online_update(running, query_block, key_block, value_block, visible):
    best, denom, accum = running
    scores = jnp.einsum(
        "qkgd,nkd->qkgn", query_block, key_block, preferred_element_type=jnp.float32
    ) / math.sqrt(HEAD_SIZE)
    shown = visible[:, None, None, :]
    scores = jnp.where(shown, scores, masked_score)
    best_next = jnp.maximum(best, jnp.max(scores, axis=-1))
    weights = jnp.where(shown, jnp.exp(scores - best_next[..., None]), 0.0)
    rescale = jnp.exp(best - best_next)
    denom = denom * rescale + jnp.sum(weights, axis=-1)
    accum = accum * rescale[..., None] + jnp.einsum(
        "qkgn,nkd->qkgd",
        weights.astype(jnp.bfloat16),
        value_block,
        preferred_element_type=jnp.float32,
    )
    return (best_next, denom, accum)


def finish_running(running):
    best, denom, accum = running
    result = accum / denom[..., None]
    return result.reshape(result.shape[0], -1).astype(jnp.bfloat16)


def attend_local(grouped_queries, key_heads, value_head_rows, segment_ids):
    sequence_total = grouped_queries.shape[0]
    kv_count = grouped_queries.shape[1]
    group_count = grouped_queries.shape[2]
    block = min(512, sequence_total)
    block_count = sequence_total // block

    def one_block(block_index, finished):
        first_row = block_index * block
        query_block = lax.dynamic_slice_in_dim(grouped_queries, first_row, block, 0)
        query_segs = lax.dynamic_slice_in_dim(segment_ids, first_row, block, 0)
        query_ids = first_row + jnp.arange(block, dtype=jnp.int32)

        def key_step(key_index, running):
            first_key = key_index * block
            key_block = lax.dynamic_slice_in_dim(key_heads, first_key, block, 0)
            value_block = lax.dynamic_slice_in_dim(value_head_rows, first_key, block, 0)
            key_segs = lax.dynamic_slice_in_dim(segment_ids, first_key, block, 0)
            key_ids = first_key + jnp.arange(block, dtype=jnp.int32)
            visible = (key_ids[None, :] <= query_ids[:, None]) & (
                key_segs[None, :] == query_segs[:, None]
            )
            return online_update(running, query_block, key_block, value_block, visible)

        running = lax.fori_loop(
            0, block_index + 1, key_step, empty_running(block, kv_count, group_count)
        )
        return lax.dynamic_update_slice_in_dim(finished, finish_running(running), first_row, 0)

    finished = jnp.zeros((sequence_total, kv_count * group_count * HEAD_SIZE), jnp.bfloat16)
    return lax.fori_loop(0, block_count, one_block, finished)


def on_device(query_states, projected_keys, projected_values, positions, segments):
    token_rows = query_states.shape[1]
    cosine_table, sine_table = yarn_tables(positions[0], HEAD_SIZE)
    cosine_table = cosine_table[:, None, :]
    sine_table = sine_table[:, None, :]
    rotated_queries = apply_rotation(
        query_states[0].astype(jnp.float32).reshape(token_rows, QUERY_HEADS, HEAD_SIZE),
        cosine_table,
        sine_table,
    ).astype(jnp.bfloat16)
    rotated_keys = apply_rotation(
        projected_keys[0].astype(jnp.float32).reshape(token_rows, KEY_VALUE_HEADS, HEAD_SIZE),
        cosine_table,
        sine_table,
    ).astype(jnp.bfloat16)
    value_head_rows = projected_values[0].reshape(token_rows, KEY_VALUE_HEADS, HEAD_SIZE)
    segment_ids = segments[0]
    row_width = lax.axis_size("seq")
    per_device = QUERY_HEADS // row_width
    key_value_local = max(1, KEY_VALUE_HEADS // row_width)
    repeat_count = max(1, row_width // KEY_VALUE_HEADS)
    query_send = rotated_queries.reshape(token_rows, row_width, per_device * HEAD_SIZE)
    key_send = jnp.broadcast_to(
        rotated_keys.reshape(
            token_rows, KEY_VALUE_HEADS // key_value_local, 1, key_value_local * HEAD_SIZE
        ),
        (token_rows, KEY_VALUE_HEADS // key_value_local, repeat_count, key_value_local * HEAD_SIZE),
    ).reshape(token_rows, row_width, key_value_local * HEAD_SIZE)
    value_send = jnp.broadcast_to(
        value_head_rows.reshape(
            token_rows, KEY_VALUE_HEADS // key_value_local, 1, key_value_local * HEAD_SIZE
        ),
        (token_rows, KEY_VALUE_HEADS // key_value_local, repeat_count, key_value_local * HEAD_SIZE),
    ).reshape(token_rows, row_width, key_value_local * HEAD_SIZE)
    segment_send = jnp.broadcast_to(
        segment_ids.astype(jnp.bfloat16)[:, None, None], (token_rows, row_width, 1)
    )
    query_all, key_all, value_all, segment_all = (
        lax.all_to_all(query_send, "seq", split_axis=1, concat_axis=0, tiled=True),
        lax.all_to_all(key_send, "seq", split_axis=1, concat_axis=0, tiled=True),
        lax.all_to_all(value_send, "seq", split_axis=1, concat_axis=0, tiled=True),
        lax.all_to_all(segment_send, "seq", split_axis=1, concat_axis=0, tiled=True),
    )
    sequence_total = token_rows * row_width
    heads_out = attend_local(
        query_all.reshape(
            sequence_total, key_value_local, per_device // key_value_local, HEAD_SIZE
        ),
        key_all.reshape(sequence_total, key_value_local, HEAD_SIZE),
        value_all.reshape(sequence_total, key_value_local, HEAD_SIZE),
        segment_all.reshape(sequence_total).astype(jnp.int32),
    )
    rows_out = lax.all_to_all(
        heads_out.reshape(sequence_total, 1, per_device * HEAD_SIZE),
        "seq",
        split_axis=0,
        concat_axis=1,
        tiled=True,
    )
    rows_out = rows_out.reshape(token_rows, QUERY_HEADS * HEAD_SIZE)
    rows_out = passed_along(rows_out, "pipe", 1)
    return rows_out[None]


def solution(mesh):
    placed = (
        P(("dp", "pipe"), "seq", None),
        P(("dp", "pipe"), "seq", None),
        P(("dp", "pipe"), "seq", None),
        P(("dp", "pipe"), "seq"),
        P(("dp", "pipe"), "seq"),
    )
    return jax.shard_map(
        on_device,
        mesh=mesh,
        in_specs=placed,
        out_specs=P(("dp", "pipe"), "seq", None),
        check_vma=False,
    )
```

profile of v0, /device:TPU:0, one launch (start us, length us, event | category | flops | bytes accessed | tf_op | source)
XLA Modules:
  0.0 201.0 jit_solution(10546775687055647915)
XLA Ops:
  0.0 0.8 convert_bitcast_fusion.1
  0.8 0.6 broadcast_in_dim.51
  1.4 6.3 %all-to-all-start = ((bf16[128,4,1]{0,2,1:T(2,128)(2,1)}), bf16[128,4,1]{0,2,1:T(2,128)(2,1)S(1)}, u32[]{:S(2)}, u32[]{:S(2)}) async-start(bf16[128,4,1]{0,2,1:T(2,128)(2,1)} %broadcast_in_dim.51), calls=%async_computation | async-start | bytes 4096 | tf_op jit(solution)/shard_map/all_to_all | solution.py:173
  7.8 0.7 convert_bitcast_fusion
  8.4 1.1 copy.44
  9.8 0.7 pad_maximum_fusion.1
  10.5 2.8 %all-to-all-done = bf16[128,4,1]{0,2,1:T(2,128)(2,1)S(1)} async-done(((bf16[128,4,1]{0,2,1:T(2,128)(2,1)}), bf16[128,4,1]{0,2,1:T(2,128)(2,1)S(1)}, u32[]{:S(2)}, u32[]{:S(2)}) %all-to-all-start) | async-done | bytes 1056 | tf_op jit(solution)/shard_map/all_to_all | solution.py:173
  13.3 3.4 %all-to-all-start.1 = ((bf16[128,4,256]{0,2,1:T(8,128)(2,1)}), bf16[128,4,256]{0,2,1:T(8,128)(2,1)S(1)}, u32[]{:S(2)}, u32[]{:S(2)}) async-start(bf16[128,4,256]{0,2,1:T(8,128)(2,1)} %bitcast.8), calls=%async_computation.1 | async-start | bytes 524288 | tf_op jit(solution)/shard_map/all_to_all | solution.py:171
  16.7 2.9 %copy.46 = f32[1,128,8192]{1,2,0:T(8,128)} copy(bf16[1,128,8192]{2,1,0:T(8,128)(2,1)S(1)} %copy-done) | data formatting | bytes 6291456 | tf_op jit(solution)/shard_map/convert_element_type | solution.py:138
  19.7 0.8 copy.50
  20.5 3.3 %all-to-all-done.1 = bf16[128,4,256]{0,2,1:T(8,128)(2,1)S(1)} async-done(((bf16[128,4,256]{0,2,1:T(8,128)(2,1)}), bf16[128,4,256]{0,2,1:T(8,128)(2,1)S(1)}, u32[]{:S(2)}, u32[]{:S(2)}) %all-to-all-start.1) | async-done | bytes 262176 | tf_op jit(solution)/shard_map/all_to_all | solution.py:171
  23.8 3.4 %all-to-all-start.3 = ((bf16[128,4,256]{0,2,1:T(8,128)(2,1)}), bf16[128,4,256]{0,2,1:T(8,128)(2,1)S(1)}, u32[]{:S(2)}, u32[]{:S(2)}) async-start(bf16[128,4,256]{0,2,1:T(8,128)(2,1)} %bitcast.17), calls=%async_computation.3 | async-start | bytes 524288 | tf_op jit(solution)/shard_map/all_to_all | solution.py:172
  27.2 2.8 %subtract_convert_fusion = (bf16[128,64,64]{0,2,1:T(8,128)(2,1)S(1)}, bf16[128,64,64]{0,2,1:T(8,128)(2,1)S(1)}) fusion(f32[128,64,128]{0,2,1:T(8,128)} %bitcast.64, f32[128,64]{0,1:T(8,128)S(1)} %get-tuple-element.110, f32[128,64]{0,1:T(8,128)S(1)} %get-tuple-element.109), kind=kLoop, calls=%fused_computation.14 | loop fusion | flops 4194304 | bytes 6356992 | tf_op jit(solution)/shard_map/convert.5
  30.0 1.5 pad_maximum_fusion
  31.6 2.4 %all-to-all-done.3 = bf16[128,4,256]{0,2,1:T(8,128)(2,1)S(1)} async-done(((bf16[128,4,256]{0,2,1:T(8,128)(2,1)}), bf16[128,4,256]{0,2,1:T(8,128)(2,1)S(1)}, u32[]{:S(2)}, u32[]{:S(2)}) %all-to-all-start.3) | async-done | bytes 262176 | tf_op jit(solution)/shard_map/all_to_all | solution.py:172
  33.9 3.6 %all-to-all-start.2 = ((bf16[128,4,2048]{0,2,1:T(8,128)(2,1)}), bf16[128,4,2048]{0,2,1:T(8,128)(2,1)S(1)}, u32[]{:S(2)}, u32[]{:S(2)}) async-start(bf16[128,4,2048]{0,2,1:T(8,128)(2,1)} %bitcast.13), calls=%async_computation.2 | async-start | bytes 4194304 | tf_op jit(solution)/shard_map/all_to_all | solution.py:170
  38.3 43.6 %all-to-all-done.2 = bf16[128,4,2048]{0,2,1:T(8,128)(2,1)S(1)} async-done(((bf16[128,4,2048]{0,2,1:T(8,128)(2,1)}), bf16[128,4,2048]{0,2,1:T(8,128)(2,1)S(1)}, u32[]{:S(2)}, u32[]{:S(2)}) %all-to-all-start.2) | async-done | bytes 2097184 | tf_op jit(solution)/shard_map/all_to_all | solution.py:170
  82.0 2.6 %copy.47 = bf16[4,128,1,2048]{3,1,0,2:T(8,128)(2,1)} copy(bf16[4,128,1,2048]{1,3,0,2:T(8,128)(2,1)S(1)} %bitcast.67) | data formatting | bytes 4194304 | tf_op jit(solution)/shard_map/all_to_all | solution.py:170
  84.6 2.2 %copy.62 = bf16[64,8,16,128]{3,2,1,0:T(8,128)(2,1)S(1)} copy(bf16[64,8,16,128]{3,1,2,0:T(8,128)(2,1)} %bitcast.68) | data formatting | bytes 4194304
  86.8 3.8 %fusion = (f32[512,2,8]{0,2,1:T(8,128)S(1)}, f32[2,512,512,8]{2,1,3,0:T(8,128)S(1)}) fusion(pred[512,512]{0,1:T(8,128)(4,1)S(1)} %fusion.12, bf16[512,2,8,128]{3,2,1,0:T(8,128)(2,1)S(1)} %bitcast.65, bf16[512,2,128,1]{2,1,0,3:T(2,128)(2,1)S(1)} %bitcast.73), kind=kOutput, calls=%fused_computation.2 | convolution fusion | flops 1086316544 | bytes 19431424 | tf_op jit(solution)/shard_map/while/body/eval_jaxpr/while/body/qkgd,nkd->qkgn/dot_general | solution.py:75
  90.6 4.0 %fusion.1 = f32[512,2,8]{0,2,1:T(8,128)S(1)} fusion(f32[2,512,512,8]{2,1,3,0:T(8,128)S(1)} %get-tuple-element.112, f32[512,2,8]{0,2,1:T(8,128)S(1)} %broadcast_maximum_fusion, pred[512,512]{0,1:T(8,128)(4,1)S(1)} %fusion.12), kind=kLoop, calls=%fused_computation.3 | loop fusion | flops 20963328 | bytes 17104896 | tf_op jit(solution)/shard_map/while/body/eval_jaxpr/while/body/reduce_sum | solution.py:83
  94.6 6.0 %fusion.7 = bf16[512,2,8,128]{0,3,2,1:T(8,128)(2,1)} fusion(f32[2,512,512,8]{2,1,3,0:T(8,128)S(1)} %get-tuple-element.112, f32[512,2,8]{0,2,1:T(8,128)S(1)} %broadcast_maximum_fusion, pred[512,512]{0,1:T(8,128)(4,1)S(1)} %fusion.12, f32[512,2,8]{0,2,1:T(8,128)S(1)} %get-tuple-element.108, f32[512,2,8]{0,2,1:T(8,128)S(1)} %get-tuple-element.107, ...), kind=kOutput, calls=%fused_computation.9 | convolution fusion | flops 1097859072 | bytes 19496960 | tf_op jit(solution)/shard_map/while/body/eval_jaxpr/while/body/qkgn,nkd->qkgd/dot_general | solution.py:84
  100.7 0.5 broadcast.185
  101.2 3.8 %reduce = bf16[512,2048]{0,1:T(8,128)(2,1)S(1)} reduce(bf16[512,1,2048]{0,2,1:T(8,128)(2,1)} %bitcast.69, bf16[]{:T(256)} %broadcast.185), dimensions={1}, to_apply=%copy.53.reduce_sub_computation | reduce | bytes 4194306 | tf_op jit(solution)/shard_map/while/body/eval_jaxpr/convert_element_type | solution.py:96
  105.0 2.4 %copy.71 = bf16[512,2048]{1,0:T(8,128)(2,1)} copy(bf16[512,2048]{0,1:T(8,128)(2,1)S(1)} %reduce) | data formatting | bytes 4194304
  107.4 4.5 %reshape.194 = bf16[4,2,131072]{2,1,0:T(2,128)(2,1)} reshape(bf16[512,2048]{1,0:T(8,128)(2,1)} %copy.71) | data formatting | bytes 4194304
  111.9 51.3 %all_to_all.69 = bf16[4,2,131072]{2,1,0:T(2,128)(2,1)S(1)} all-to-all(bf16[4,2,131072]{2,1,0:T(2,128)(2,1)} %reshape.194), channel_id=1, replica_groups=mesh['dp'=2,'pipe'=4,'seq'=4] {'seq'}, dimensions={0} | all-to-all | bytes 4194304 | tf_op jit(solution)/shard_map/all_to_all | solution.py:184
  163.2 3.4 %reshape.195 = bf16[512,1,2048]{2,1,0:T(2,128)(2,1)} reshape(bf16[4,2,131072]{2,1,0:T(2,128)(2,1)S(1)} %all_to_all.69) | data formatting | bytes 4194304
  166.5 3.5 %copy.61 = bf16[512,1,2048]{2,0,1:T(8,128)(2,1)S(1)} copy(bf16[512,1,2048]{2,1,0:T(2,128)(2,1)} %reshape.195) | data formatting | bytes 4194304
  170.0 2.5 %copy.54 = bf16[128,4,1,2048]{0,3,1,2:T(8,128)(2,1)} copy(bf16[128,4,1,2048]{3,0,1,2:T(8,128)(2,1)S(1)} %bitcast.66) | data formatting | bytes 4194304 | tf_op jit(solution)/shard_map/all_to_all | solution.py:184
  172.5 25.7 %collective-permute-done = bf16[128,8192]{0,1:T(8,128)(2,1)S(1)} collective-permute-done((bf16[128,8192]{0,1:T(8,128)(2,1)}, bf16[128,8192]{0,1:T(8,128)(2,1)S(1)}, u32[]{:S(2)}, u32[]{:S(2)}) %collective-permute-start) | collective-permute-done | bytes 2097184 | tf_op jit(solution)/shard_map/ppermute | solution.py:24
  198.2 2.9 %copy.55 = bf16[1,128,8192]{2,1,0:T(8,128)(2,1)} copy(bf16[1,128,8192]{1,2,0:T(8,128)(2,1)S(1)} %bitcast.71) | data formatting | bytes 4194304 | tf_op jit(solution)/shard_map/broadcast_in_dim | solution.py:193
  (16 shorter events, 1.1 us)
Async XLA Ops:
  0.0 16.7 %copy-start = (bf16[1,128,8192]{2,1,0:T(8,128)(2,1)S(1)}, bf16[1,128,8192]{2,1,0:T(8,128)(2,1)}, u32[]{:S(2)}) copy-start(bf16[1,128,8192]{2,1,0:T(8,128)(2,1)} %param.5) | copy-start | bytes 6291460
  1.4 11.9 %all-to-all-start = ((bf16[128,4,1]{0,2,1:T(2,128)(2,1)}), bf16[128,4,1]{0,2,1:T(2,128)(2,1)S(1)}, u32[]{:S(2)}, u32[]{:S(2)}) async-start(bf16[128,4,1]{0,2,1:T(2,128)(2,1)} %broadcast_in_dim.51), calls=%async_computation | async-start | bytes 4096 | tf_op jit(solution)/shard_map/all_to_all | solution.py:173
  9.5 10.2 %copy-start.1 = (bf16[1,128,1024]{2,1,0:T(8,128)(2,1)S(1)}, bf16[1,128,1024]{2,1,0:T(8,128)(2,1)}, u32[]{:S(2)}) copy-start(bf16[1,128,1024]{2,1,0:T(8,128)(2,1)} %param.7) | copy-start | bytes 786436
  13.3 10.5 %all-to-all-start.1 = ((bf16[128,4,256]{0,2,1:T(8,128)(2,1)}), bf16[128,4,256]{0,2,1:T(8,128)(2,1)S(1)}, u32[]{:S(2)}, u32[]{:S(2)}) async-start(bf16[128,4,256]{0,2,1:T(8,128)(2,1)} %bitcast.8), calls=%async_computation.1 | async-start | bytes 524288 | tf_op jit(solution)/shard_map/all_to_all | solution.py:171
  23.8 10.2 %all-to-all-start.3 = ((bf16[128,4,256]{0,2,1:T(8,128)(2,1)}), bf16[128,4,256]{0,2,1:T(8,128)(2,1)S(1)}, u32[]{:S(2)}, u32[]{:S(2)}) async-start(bf16[128,4,256]{0,2,1:T(8,128)(2,1)} %bitcast.17), calls=%async_computation.3 | async-start | bytes 524288 | tf_op jit(solution)/shard_map/all_to_all | solution.py:172
  33.9 48.0 %all-to-all-start.2 = ((bf16[128,4,2048]{0,2,1:T(8,128)(2,1)}), bf16[128,4,2048]{0,2,1:T(8,128)(2,1)S(1)}, u32[]{:S(2)}, u32[]{:S(2)}) async-start(bf16[128,4,2048]{0,2,1:T(8,128)(2,1)} %bitcast.13), calls=%async_computation.2 | async-start | bytes 4194304 | tf_op jit(solution)/shard_map/all_to_all | solution.py:170
  172.5 25.7 %collective-permute-start = (bf16[128,8192]{0,1:T(8,128)(2,1)}, bf16[128,8192]{0,1:T(8,128)(2,1)S(1)}, u32[]{:S(2)}, u32[]{:S(2)}) collective-permute-start(bf16[128,8192]{0,1:T(8,128)(2,1)} %bitcast.70), channel_id=1, source_target_pairs={{12,0},{0,4},{4,8},{8,12},{13,1},{1,5},{5,9},{9,13},{14,2},{2,6},{... | collective-permute-start | bytes 6291464 | tf_op jit(solution)/shard_map/ppermute | solution.py:24
where the time goes:
time: 202 us; the launch traced here: 201 us
  waiting for transfers between devices  77.8 us (39%)
  blocking collectives  51.3 us (25%)
  local copies, waits for them, and re-layouts  30.3 us (15%)
  starting transfers between devices  16.8 us (8%)
  other arithmetic  14.9 us (7%)
  matrix products  9.84 us (5%)
    all_to_all x1, blocking collectives, on_device(): lax.all_to_all(heads_out.reshape(sequence_total, 1, per_device * HEAD_SIZ...  51.3 us
    all_to_all x1, waiting for transfers between devices, on_device(): lax.all_to_all(query_send, 'seq', split_axis=1, concat_axis=0, tiled=True)  43.6 us
    ppermute x1, waiting for transfers between devices, passed_along(): return lax.ppermute(block, axis, route)  25.7 us
    unnamed x10, local copies, waits for them, and re-layouts  16.7 us
    all_to_all x1, starting transfers between devices, on_device(): lax.all_to_all(segment_send, 'seq', split_axis=1, concat_axis=0, tiled=True)  6.35 us
    dot_general x1, matrix products, online_update(): jnp.einsum('qkgn,nkd->qkgd', weights.astype(jnp.bfloat16), value_block, p...  6.04 us
  transfers between devices with their start and end apart: 5, of which 5 were waited for; matrix products, arithmetic and copies ran while one was open for 6% of the time, Pallas kernels for 0%

commit v1 on v0

v1 whole, which is shorter than its diff:
```python
import functools
import math

import jax
import jax.numpy as jnp
from jax import lax
from jax.experimental import pallas as pl
from jax.experimental.pallas import tpu as pltpu
from jax.sharding import PartitionSpec as P

QUERY_HEADS = 64
KEY_VALUE_HEADS = 8
HEAD_SIZE = 128
GROUP = QUERY_HEADS // KEY_VALUE_HEADS
WIDTH = GROUP * HEAD_SIZE
SEGMENT_ROWS = 16

rope_theta = 1000000.0
yarn_factor = 4.0
trained_length = 32768.0
fast_beta = 32.0
slow_beta = 1.0
masked_score = -1e30


def yarn_tables(positions, head_dim):
    half_dim = head_dim // 2
    pair_index = jnp.arange(half_dim, dtype=jnp.float32)
    base_freq = 1.0 / rope_theta ** (2.0 * pair_index / head_dim)
    lower = math.floor(
        head_dim
        * math.log(trained_length / (fast_beta * 2.0 * math.pi))
        / (2.0 * math.log(rope_theta))
    )
    upper = math.ceil(
        head_dim
        * math.log(trained_length / (slow_beta * 2.0 * math.pi))
        / (2.0 * math.log(rope_theta))
    )
    lower = max(lower, 0)
    upper = min(upper, head_dim - 1)
    upper = max(upper, lower + 1)
    ramp_value = jnp.clip((pair_index - lower) / (upper - lower), 0.0, 1.0)
    keep_share = 1.0 - ramp_value
    inv_freq = base_freq / yarn_factor * (1.0 - keep_share) + base_freq * keep_share
    attn_gain = 0.1 * math.log(yarn_factor) + 1.0
    angles = positions.astype(jnp.float32)[..., None] * inv_freq
    return (jnp.cos(angles) * attn_gain, jnp.sin(angles) * attn_gain)


def rotated(states, cosine, sine):
    wide = states.astype(jnp.float32)
    return (wide * cosine + pltpu.roll(wide, HEAD_SIZE // 2, 1) * sine).astype(jnp.bfloat16)


def wide_tables(cos_ref, sin_ref):
    cosine, sine = cos_ref[...], sin_ref[...]
    return jnp.concatenate([cosine, cosine], axis=1), jnp.concatenate([-sine, sine], axis=1)


def pack_kernel(groups, keys_ref, values_ref, segment_ref, cos_ref, sin_ref, *packed):
    cosine, sine = wide_tables(cos_ref, sin_ref)
    rows = keys_ref.shape[0]
    ids = segment_ref[...].astype(jnp.float32).astype(jnp.bfloat16)
    first = 0
    for count, out_ref in zip(groups, packed):
        for g in range(count):
            columns = slice((first + g) * HEAD_SIZE, (first + g + 1) * HEAD_SIZE)
            out_ref[g * rows : (g + 1) * rows, :] = rotated(keys_ref[:, columns], cosine, sine)
            out_ref[(count + g) * rows : (count + g + 1) * rows, :] = values_ref[:, columns]
        out_ref[2 * count * rows :, :] = jnp.broadcast_to(ids, (SEGMENT_ROWS, rows))
        first += count


def pack(groups, keys, values, segments, cosine, sine):
    rows = keys.shape[0]
    return pl.pallas_call(
        functools.partial(pack_kernel, groups),
        out_shape=[
            jax.ShapeDtypeStruct((2 * g * rows + SEGMENT_ROWS, HEAD_SIZE), jnp.bfloat16)
            for g in groups
        ],
        name="pack",
        cost_estimate=pl.CostEstimate(
            flops=8 * keys.size, bytes_accessed=8 * keys.size, transcendentals=0
        ),
    )(keys, values, segments, cosine, sine)


def rotate_kernel(queries_ref, cos_ref, sin_ref, out_ref):
    cosine, sine = wide_tables(cos_ref, sin_ref)
    for h in range(GROUP):
        columns = slice(h * HEAD_SIZE, (h + 1) * HEAD_SIZE)
        out_ref[:, columns] = rotated(queries_ref[:, columns], cosine, sine)


def rotate(queries, first, count, cosine, sine):
    rows = queries.shape[0]
    return pl.pallas_call(
        rotate_kernel,
        grid=(count,),
        in_specs=[
            pl.BlockSpec((rows, WIDTH), lambda g: (0, first + g)),
            pl.BlockSpec((rows, HEAD_SIZE // 2), lambda g: (0, 0)),
            pl.BlockSpec((rows, HEAD_SIZE // 2), lambda g: (0, 0)),
        ],
        out_specs=pl.BlockSpec((rows, WIDTH), lambda g: (0, g)),
        out_shape=jax.ShapeDtypeStruct((rows, count * WIDTH), jnp.bfloat16),
        name="rotate",
        cost_estimate=pl.CostEstimate(
            flops=4 * rows * count * WIDTH,
            bytes_accessed=4 * rows * count * WIDTH,
            transcendentals=0,
        ),
    )(queries, cosine, sine)


def attend_kernel(
    before, after, count, blocks, here_ref, *refs
):
    ready = refs[: (before > 0) + (after > 0)]
    refs = refs[len(ready) :]
    queries_ref, payloads = refs[0], refs[1 : 1 + blocks]
    out_ref, bias_ref, keys_ref, values_ref, scores_ref = refs[1 + blocks :]
    step = pl.program_id(0)
    rows = queries_ref.shape[0]
    segment_row = 2 * count * rows

    @pl.when(step == 0)
    def _():
        here = here_ref[0]
        own = payloads[0][segment_row : segment_row + 1, :].astype(jnp.float32)
        query_ids = jnp.broadcast_to(own, (rows, rows)).T
        row = lax.broadcasted_iota(jnp.int32, (rows, rows), 0)
        lane = lax.broadcasted_iota(jnp.int32, (rows, rows), 1)
        for b in range(blocks):
            ids = payloads[b][segment_row : segment_row + 1, :].astype(jnp.float32)
            visible = query_ids == jnp.broadcast_to(ids, (rows, rows))
            ahead = jnp.where(here >= b, -b * rows, (blocks - b) * rows)
            visible = visible & (lane + ahead <= row)
            bias_ref[:, b * rows : (b + 1) * rows] = jnp.where(visible, 0.0, masked_score)

    active = (step >= before) & (step < before + count)

    @pl.when(active)
    def _():
        g = step - before
        for b in range(blocks):
            first = pl.multiple_of(g * rows, rows)
            keys_ref[b * rows : (b + 1) * rows, :] = payloads[b][pl.ds(first, rows), :]
            first = pl.multiple_of((count + g) * rows, rows)
            values_ref[b * rows : (b + 1) * rows, :] = payloads[b][pl.ds(first, rows), :]
        keys = keys_ref[...]
        values = values_ref[...]
        scale = 1.0 / math.sqrt(HEAD_SIZE)
        for h in range(GROUP):
            columns = slice(h * HEAD_SIZE, (h + 1) * HEAD_SIZE)
            scores = lax.dot_general(
                queries_ref[:, columns],
                keys,
                (((1,), (1,)), ((), ())),
                preferred_element_type=jnp.float32,
            )
            scores = scores * scale + bias_ref[...]
            best = jnp.max(scores, axis=1, keepdims=True)
            weights = jnp.exp(scores - best)
            totals = jnp.sum(weights, axis=1, keepdims=True)
            summed = jnp.dot(
                weights.astype(jnp.bfloat16), values, preferred_element_type=jnp.float32
            )
            out_ref[:, columns] = (summed / totals).astype(jnp.bfloat16)

    if before:

        @pl.when(step < before)
        def _():
            out_ref[...] = ready[0][...]

    if after:

        @pl.when(step >= before + count)
        def _():
            out_ref[...] = ready[-1][...]


def attend(queries, payloads, here, ready_before=None, ready_after=None):
    rows = queries.shape[0]
    count = queries.shape[1] // WIDTH
    blocks = len(payloads)
    before = 0 if ready_before is None else ready_before.shape[1] // WIDTH
    after = 0 if ready_after is None else ready_after.shape[1] // WIDTH
    total = before + count + after
    ready, ready_specs = [], []
    if before:
        ready.append(ready_before)
        ready_specs.append(pl.BlockSpec((rows, WIDTH), lambda g, s: (0, jnp.minimum(g, before - 1))))
    if after:
        ready.append(ready_after)
        ready_specs.append(
            pl.BlockSpec((rows, WIDTH), lambda g, s: (0, jnp.maximum(g - before - count, 0)))
        )
    keys = blocks * rows
    return pl.pallas_call(
        functools.partial(attend_kernel, before, after, count, blocks),
        grid_spec=pltpu.PrefetchScalarGridSpec(
            num_scalar_prefetch=1,
            grid=(total,),
            in_specs=[
                *ready_specs,
                pl.BlockSpec((rows, WIDTH), lambda g, s: (0, jnp.clip(g - before, 0, count - 1))),
                *[pl.BlockSpec(p.shape, lambda g, s: (0, 0)) for p in payloads],
            ],
            out_specs=pl.BlockSpec((rows, WIDTH), lambda g, s: (0, g)),
            scratch_shapes=[
                pltpu.VMEM((rows, keys), jnp.float32),
                pltpu.VMEM((keys, HEAD_SIZE), jnp.bfloat16),
                pltpu.VMEM((keys, HEAD_SIZE), jnp.bfloat16),
                pltpu.VMEM((rows, keys), jnp.float32),
            ],
        ),
        out_shape=jax.ShapeDtypeStruct((rows, total * WIDTH), jnp.bfloat16),
        name="attend",
        cost_estimate=pl.CostEstimate(
            flops=4 * rows * keys * count * WIDTH,
            bytes_accessed=4 * rows * count * WIDTH,
            transcendentals=rows * keys * count * GROUP,
        ),
    )(here, *ready, queries, *payloads)


def ring(block, axis):
    size = lax.axis_size(axis)
    return lax.ppermute(block, axis, [(i, (i + 1) % size) for i in range(size)])


CHUNKS = (4, 4)


def on_device(query_states, projected_keys, projected_values, positions, segments):
    cosine, sine = yarn_tables(positions[0], HEAD_SIZE)
    here = lax.axis_index("seq").astype(jnp.int32).reshape(1)
    size = lax.axis_size("seq")
    stay, move = CHUNKS
    pay_stay, pay_move = pack(
        CHUNKS, projected_keys[0], projected_values[0], segments, cosine, sine
    )
    pay_move = ring(pay_move, "pipe")
    stay_blocks, move_blocks = [pay_stay], [pay_move]
    queries_stay = rotate(query_states[0], 0, stay, cosine, sine)
    queries_move = ring(rotate(query_states[0], stay, move, cosine, sine), "pipe")
    for _ in range(size - 1):
        stay_blocks.append(ring(stay_blocks[-1], "seq"))
    for _ in range(size - 1):
        move_blocks.append(ring(move_blocks[-1], "seq"))
    out_stay = ring(attend(queries_stay, stay_blocks, here), "pipe")
    return attend(queries_move, move_blocks, here, ready_before=out_stay)[None]


def solution(mesh):
    placed = (
        P(("dp", "pipe"), "seq", None),
        P(("dp", "pipe"), "seq", None),
        P(("dp", "pipe"), "seq", None),
        P(("dp", "pipe"), "seq"),
        P(("dp", "pipe"), "seq"),
    )
    return jax.shard_map(
        on_device,
        mesh=mesh,
        in_specs=placed,
        out_specs=P(("dp", "pipe"), "seq", None),
        check_vma=False,
    )
```

time: 202 us -> 91.7 us (0.45)
  blocking collectives: 51.3 us -> 0 us
  Pallas kernels: 0 us -> 34.3 us
  waiting for transfers between devices: 77.8 us -> 48.5 us
  local copies, waits for them, and re-layouts: 30.3 us -> 2.35 us
  other arithmetic: 14.9 us -> 1.65 us
  starting transfers between devices: 16.8 us -> 4.45 us
  matrix products: 9.84 us -> 0 us
    all_to_all x4 -> x0, waiting for transfers between devices: 52.1 us -> none  [the longest x1 43.6 us: on_device(): lax.all_to_all(query_send, 'seq', split_axis=1, concat_axis=0, tiled=True)]
    all_to_all x1 -> x0, blocking collectives: 51.3 us -> none  [on_device(): lax.all_to_all(heads_out.reshape(sequence_total, 1, per_device * HEAD_SIZ...]
    pallas_call x0 -> x5, Pallas kernels: none -> 34.3 us  [the longest x2 24.6 us: attend(): pl.pallas_call(functools.partial(attend_kernel, before, after, count, blo...]
    ppermute x1 -> x9, waiting for transfers between devices: 25.7 us -> 48.5 us  [ring(): return lax.ppermute(block, axis, [(i, (i + 1) % size) for i in range(size)])]
    all_to_all x4 -> x0, starting transfers between devices: 16.8 us -> none  [the longest x1 6.35 us: on_device(): lax.all_to_all(segment_send, 'seq', split_axis=1, concat_axis=0, tiled=True)]
    unnamed x10 -> x18, local copies, waits for them, and re-layouts: 16.7 us -> 2.35 us
    dot_general x2 -> x0, matrix products: 9.84 us -> none  [the longest x1 6.04 us: online_update(): jnp.einsum('qkgn,nkd->qkgd', weights.astype(jnp.bfloat16), value_block, p...]
    all_to_all x4 -> x0, local copies, waits for them, and re-layouts: 5.43 us -> none  [the longest x1 2.58 us: on_device(): lax.all_to_all(query_send, 'seq', split_axis=1, concat_axis=0, tiled=True)]
  transfers between devices with their start and end apart: 5 -> 9, of which waited for: 5 -> 5; matrix products, arithmetic and copies ran while one was open for 6% -> 0% of each run, Pallas kernels for 0% -> 21%
where the time goes in v1:
time: 91.7 us; the launch traced here: 91.3 us
  waiting for transfers between devices  48.5 us (53%)
  Pallas kernels  34.3 us (37%)
  starting transfers between devices  4.45 us (5%)
  local copies, waits for them, and re-layouts  2.35 us (3%)
  other arithmetic  1.65 us (2%)
    ppermute x9, waiting for transfers between devices, ring(): return lax.ppermute(block, axis, [(i, (i + 1) % size) for i in range(size)])  48.5 us
    pallas_call x2, Pallas kernels, attend(): pl.pallas_call(functools.partial(attend_kernel, before, after, count, blo...  24.6 us
    pallas_call x2, Pallas kernels, rotate(): pl.pallas_call(rotate_kernel, grid=(count,), in_specs=[pl.BlockSpec((rows...  7.64 us
    ppermute x9, starting transfers between devices, ring(): return lax.ppermute(block, axis, [(i, (i + 1) % size) for i in range(size)])  4.45 us
    unnamed x18, local copies, waits for them, and re-layouts  2.35 us
    pallas_call x1, Pallas kernels, pack(): pl.pallas_call(functools.partial(pack_kernel, groups), out_shape=[jax.Sha...  2.04 us
  transfers between devices with their start and end apart: 9, of which 5 were waited for; matrix products, arithmetic and copies ran while one was open for 0% of the time, Pallas kernels for 21%

profile of v1, /device:TPU:0, one launch (start us, length us, event | category | flops | bytes accessed | tf_op | source)
XLA Modules:
  0.0 91.3 jit_solution(2199378713789758773)
XLA Ops:
  0.0 0.7 convert_bitcast_fusion
  0.7 1.0 %fusion.1 = (f32[128,64]{1,0:T(8,128)}, f32[128,64]{1,0:T(8,128)}) fusion(f32[64]{0:T(128)S(1)} %multiply_add_fusion, f32[128]{0:T(128)S(1)} %convert_bitcast_fusion), kind=kLoop, calls=%fused_computation.3 | loop fusion | flops 24576 | bytes 66304 | tf_op jit(solution)/shard_map/mul | solution.py:48
  1.6 2.0 %pack.1 = (bf16[1040,128]{1,0:T(8,128)(2,1)}, bf16[1040,128]{1,0:T(8,128)(2,1)}) custom-call(bf16[128,1024]{1,0:T(8,128)(2,1)} %bitcast.9, bf16[128,1024]{1,0:T(8,128)(2,1)} %bitcast.10, s32[1,128]{1,0:T(1,128)} %segment_ref.1, f32[128,64]{1,0:T(8,128)} %get-tuple-element.10.cos_ref, f32[128,64]{1,0:T(8,128)} %get-tuple-element.9.sin_ref), custom_call_target="tpu_custom_call" | custom-call | flops 1048576 | bytes 1048576 | tf_op jit(solution)/shard_map/pack/pallas_call | solution.py:77
  3.7 3.1 %collective-permute-start = (bf16[1040,128]{1,0:T(8,128)(2,1)}, bf16[1040,128]{1,0:T(8,128)(2,1)S(1)}, u32[]{:S(2)}, u32[]{:S(2)}) collective-permute-start(bf16[1040,128]{1,0:T(8,128)(2,1)} %get-tuple-element.7.refs_1_), channel_id=1, source_target_pairs={{0,1},{1,2},{2,3},{3,0},{4,5},{5,6},{6,7},{7,4},{8,9},{9,10},{10,1... | collective-permute-start | bytes 798728 | tf_op jit(solution)/shard_map/ppermute | solution.py:233
  6.7 8.6 %collective-permute-done.refs_2_ = bf16[1040,128]{1,0:T(8,128)(2,1)S(1)} collective-permute-done((bf16[1040,128]{1,0:T(8,128)(2,1)}, bf16[1040,128]{1,0:T(8,128)(2,1)S(1)}, u32[]{:S(2)}, u32[]{:S(2)}) %collective-permute-start) | collective-permute-done | bytes 266272 | tf_op jit(solution)/shard_map/ppermute | solution.py:233
  15.4 0.0 collective-permute-start.1
  15.4 9.4 %collective-permute-done.1.refs_3_ = bf16[1040,128]{1,0:T(8,128)(2,1)S(1)} collective-permute-done((bf16[1040,128]{1,0:T(8,128)(2,1)S(1)}, bf16[1040,128]{1,0:T(8,128)(2,1)S(1)}, u32[]{:S(2)}, u32[]{:S(2)}) %collective-permute-start.1) | collective-permute-done | bytes 266272 | tf_op jit(solution)/shard_map/ppermute | solution.py:233
  24.7 0.0 collective-permute-start.2
  24.7 0.0 collective-permute-start.5
  24.7 3.9 %rotate.3 = bf16[128,4096]{1,0:T(8,128)(2,1)} custom-call(bf16[128,8192]{1,0:T(8,128)(2,1)} %bitcast.7, f32[128,64]{1,0:T(8,128)} %get-tuple-element.10.cos_ref, f32[128,64]{1,0:T(8,128)} %get-tuple-element.9.sin_ref), custom_call_target="tpu_custom_call" | custom-call | flops 2097152 | bytes 2097152 | tf_op jit(solution)/shard_map/rotate/pallas_call | solution.py:99
  28.6 1.3 %collective-permute-start.4 = (bf16[128,4096]{1,0:T(8,128)(2,1)}, bf16[128,4096]{1,0:T(8,128)(2,1)S(1)}, u32[]{:S(2)}, u32[]{:S(2)}) collective-permute-start(bf16[128,4096]{1,0:T(8,128)(2,1)} %rotate.3), channel_id=1, source_target_pairs={{0,4},{4,8},{8,12},{12,0},{1,5},{5,9},{9,13},{13,1},{2,6},{6,10},{... | collective-permute-start | bytes 3145736 | tf_op jit(solution)/shard_map/ppermute | solution.py:233
  29.9 3.8 %rotate.2.refs_0_ = bf16[128,4096]{1,0:T(8,128)(2,1)} custom-call(bf16[128,8192]{1,0:T(8,128)(2,1)} %bitcast.8, f32[128,64]{1,0:T(8,128)} %get-tuple-element.10.cos_ref, f32[128,64]{1,0:T(8,128)} %get-tuple-element.9.sin_ref), custom_call_target="tpu_custom_call" | custom-call | flops 2097152 | bytes 2097152 | tf_op jit(solution)/shard_map/rotate/pallas_call | solution.py:99
  33.7 0.0 collective-permute-done.2.refs_4_
  33.7 0.7 copy-done.8
  34.4 11.3 %attend.2 = bf16[128,4096]{1,0:T(8,128)(2,1)} custom-call(s32[1]{0:T(128)} %bitcast.here_ref, bf16[128,4096]{1,0:T(8,128)(2,1)} %rotate.2.refs_0_, bf16[1040,128]{1,0:T(8,128)(2,1)} %get-tuple-element.7.refs_1_, bf16[1040,128]{1,0:T(8,128)(2,1)} %copy-done.6, bf16[1040,128]{1,0:T(8,128)(2,1)} %copy-done.7, bf16[1040,128]{1,0:T(8,128)(2,1)} %copy-done.8), custom_call_target="tpu_custom_call" | custom-call | flops 1073741824 | bytes 2097152 | tf_op jit(solution)/shard_map/attend/pallas_call | solution.py:203
  45.7 0.1 collective-permute-start.3
  45.8 0.0 collective-permute-done.5.refs_2_
  45.8 0.0 collective-permute-start.6
  45.8 11.0 %collective-permute-done.6.refs_3_ = bf16[1040,128]{1,0:T(8,128)(2,1)S(1)} collective-permute-done((bf16[1040,128]{1,0:T(8,128)(2,1)S(1)}, bf16[1040,128]{1,0:T(8,128)(2,1)S(1)}, u32[]{:S(2)}, u32[]{:S(2)}) %collective-permute-start.6) | collective-permute-done | bytes 266272 | tf_op jit(solution)/shard_map/ppermute | solution.py:233
  56.8 0.0 collective-permute-start.7
  56.8 10.2 %collective-permute-done.7.refs_4_ = bf16[1040,128]{1,0:T(8,128)(2,1)S(1)} collective-permute-done((bf16[1040,128]{1,0:T(8,128)(2,1)S(1)}, bf16[1040,128]{1,0:T(8,128)(2,1)S(1)}, u32[]{:S(2)}, u32[]{:S(2)}) %collective-permute-start.7) | collective-permute-done | bytes 266272 | tf_op jit(solution)/shard_map/ppermute | solution.py:233
  67.0 0.0 collective-permute-start.8
  67.0 0.0 collective-permute-done.4.refs_1_
  67.0 0.0 copy-start
  67.0 9.3 %collective-permute-done.8.refs_5_ = bf16[1040,128]{1,0:T(8,128)(2,1)S(1)} collective-permute-done((bf16[1040,128]{1,0:T(8,128)(2,1)S(1)}, bf16[1040,128]{1,0:T(8,128)(2,1)S(1)}, u32[]{:S(2)}, u32[]{:S(2)}) %collective-permute-start.8) | collective-permute-done | bytes 266272 | tf_op jit(solution)/shard_map/ppermute | solution.py:233
  76.3 0.0 collective-permute-done.3.refs_0_
  76.3 0.0 copy-done.3
  76.4 0.0 copy-done.4
  76.4 0.0 copy-done
  76.4 0.7 copy-done.5
  77.0 1.0 %copy-done.1 = bf16[128,4096]{1,0:T(8,128)(2,1)} copy-done((bf16[128,4096]{1,0:T(8,128)(2,1)}, bf16[128,4096]{1,0:T(8,128)(2,1)S(1)}, u32[]{:S(2)}) %copy-start.1) | copy-done | bytes 1048600
  78.0 13.3 %attend.3 = bf16[128,8192]{1,0:T(8,128)(2,1)} custom-call(s32[1]{0:T(128)} %bitcast.here_ref, bf16[128,4096]{1,0:T(8,128)(2,1)} %copy-done.1, bf16[128,4096]{1,0:T(8,128)(2,1)} %copy-done, bf16[1040,128]{1,0:T(8,128)(2,1)} %copy-done.2, bf16[1040,128]{1,0:T(8,128)(2,1)} %copy-done.3, bf16[1040,128]{1,0:T(8,128)(2,1)} %copy-done.4, bf16[1040,128]{1,0:T(8,128)(2,1)} %copy-done.5), custom_call_target="tpu_custom_call" | custom-call | flops 1073741824 | bytes 2097152 | tf_op jit(solution)/shard_map/attend/pallas_call | solution.py:203
  (12 shorter events, 0.0 us)
Async XLA Ops:
  3.7 11.7 %collective-permute-start = (bf16[1040,128]{1,0:T(8,128)(2,1)}, bf16[1040,128]{1,0:T(8,128)(2,1)S(1)}, u32[]{:S(2)}, u32[]{:S(2)}) collective-permute-start(bf16[1040,128]{1,0:T(8,128)(2,1)} %get-tuple-element.7.refs_1_), channel_id=1, source_target_pairs={{0,1},{1,2},{2,3},{3,0},{4,5},{5,6},{6,7},{7,4},{8,9},{9,10},{10,1... | collective-permute-start | bytes 798728 | tf_op jit(solution)/shard_map/ppermute | solution.py:233
  15.4 18.3 %copy-start.6 = (bf16[1040,128]{1,0:T(8,128)(2,1)}, bf16[1040,128]{1,0:T(8,128)(2,1)S(1)}, u32[]{:S(2)}) copy-start(bf16[1040,128]{1,0:T(8,128)(2,1)S(1)} %collective-permute-done.refs_2_) | copy-start | bytes 798724
  15.4 9.4 %collective-permute-start.1 = (bf16[1040,128]{1,0:T(8,128)(2,1)S(1)}, bf16[1040,128]{1,0:T(8,128)(2,1)S(1)}, u32[]{:S(2)}, u32[]{:S(2)}) collective-permute-start(bf16[1040,128]{1,0:T(8,128)(2,1)S(1)} %collective-permute-done.refs_2_), channel_id=1, source_target_pairs={{0,1},{1,2},{2,3},{3,0},{4,5},{5,6},{6,7},{7,4},{8,9},{9,10},{10,1... | collective-permute-start | bytes 798728 | tf_op jit(solution)/shard_map/ppermute | solution.py:233
  24.7 8.9 %copy-start.7 = (bf16[1040,128]{1,0:T(8,128)(2,1)}, bf16[1040,128]{1,0:T(8,128)(2,1)S(1)}, u32[]{:S(2)}) copy-start(bf16[1040,128]{1,0:T(8,128)(2,1)S(1)} %collective-permute-done.1.refs_3_) | copy-start | bytes 798724
  24.7 8.9 %collective-permute-start.2 = (bf16[1040,128]{1,0:T(8,128)(2,1)S(1)}, bf16[1040,128]{1,0:T(8,128)(2,1)S(1)}, u32[]{:S(2)}, u32[]{:S(2)}) collective-permute-start(bf16[1040,128]{1,0:T(8,128)(2,1)S(1)} %collective-permute-done.1.refs_3_), channel_id=1, source_target_pairs={{0,1},{1,2},{2,3},{3,0},{4,5},{5,6},{6,7},{7,4},{8,9},{9,10},{10,1... | collective-permute-start | bytes 798728 | tf_op jit(solution)/shard_map/ppermute | solution.py:233
  24.7 21.0 %collective-permute-start.5 = (bf16[1040,128]{1,0:T(8,128)(2,1)}, bf16[1040,128]{1,0:T(8,128)(2,1)S(1)}, u32[]{:S(2)}, u32[]{:S(2)}) collective-permute-start(bf16[1040,128]{1,0:T(8,128)(2,1)} %get-tuple-element.8), channel_id=1, source_target_pairs={{0,4},{4,8},{8,12},{12,0},{1,5},{5,9},{9,13},{13,1},{2,6},{6,10},{... | collective-permute-start | bytes 798728 | tf_op jit(solution)/shard_map/ppermute | solution.py:233
  28.6 38.4 %collective-permute-start.4 = (bf16[128,4096]{1,0:T(8,128)(2,1)}, bf16[128,4096]{1,0:T(8,128)(2,1)S(1)}, u32[]{:S(2)}, u32[]{:S(2)}) collective-permute-start(bf16[128,4096]{1,0:T(8,128)(2,1)} %rotate.3), channel_id=1, source_target_pairs={{0,4},{4,8},{8,12},{12,0},{1,5},{5,9},{9,13},{13,1},{2,6},{6,10},{... | collective-permute-start | bytes 3145736 | tf_op jit(solution)/shard_map/ppermute | solution.py:233
  33.7 0.7 copy-start.8
  45.7 30.7 %collective-permute-start.3 = (bf16[128,4096]{1,0:T(8,128)(2,1)}, bf16[128,4096]{1,0:T(8,128)(2,1)S(1)}, u32[]{:S(2)}, u32[]{:S(2)}) collective-permute-start(bf16[128,4096]{1,0:T(8,128)(2,1)} %attend.2), channel_id=1, source_target_pairs={{0,4},{4,8},{8,12},{12,0},{1,5},{5,9},{9,13},{13,1},{2,6},{6,10},{... | collective-permute-start | bytes 3145736 | tf_op jit(solution)/shard_map/ppermute | solution.py:233
  45.8 30.6 %copy-start.2 = (bf16[1040,128]{1,0:T(8,128)(2,1)}, bf16[1040,128]{1,0:T(8,128)(2,1)S(1)}, u32[]{:S(2)}) copy-start(bf16[1040,128]{1,0:T(8,128)(2,1)S(1)} %collective-permute-done.5.refs_2_) | copy-start | bytes 798724
  45.8 11.0 %collective-permute-start.6 = (bf16[1040,128]{1,0:T(8,128)(2,1)S(1)}, bf16[1040,128]{1,0:T(8,128)(2,1)S(1)}, u32[]{:S(2)}, u32[]{:S(2)}) collective-permute-start(bf16[1040,128]{1,0:T(8,128)(2,1)S(1)} %collective-permute-done.5.refs_2_), channel_id=1, source_target_pairs={{0,1},{1,2},{2,3},{3,0},{4,5},{5,6},{6,7},{7,4},{8,9},{9,10},{10,1... | collective-permute-start | bytes 798728 | tf_op jit(solution)/shard_map/ppermute | solution.py:233
  56.8 19.6 %copy-start.3 = (bf16[1040,128]{1,0:T(8,128)(2,1)}, bf16[1040,128]{1,0:T(8,128)(2,1)S(1)}, u32[]{:S(2)}) copy-start(bf16[1040,128]{1,0:T(8,128)(2,1)S(1)} %collective-permute-done.6.refs_3_) | copy-start | bytes 798724
  56.8 10.2 %collective-permute-start.7 = (bf16[1040,128]{1,0:T(8,128)(2,1)S(1)}, bf16[1040,128]{1,0:T(8,128)(2,1)S(1)}, u32[]{:S(2)}, u32[]{:S(2)}) collective-permute-start(bf16[1040,128]{1,0:T(8,128)(2,1)S(1)} %collective-permute-done.6.refs_3_), channel_id=1, source_target_pairs={{0,1},{1,2},{2,3},{3,0},{4,5},{5,6},{6,7},{7,4},{8,9},{9,10},{10,1... | collective-permute-start | bytes 798728 | tf_op jit(solution)/shard_map/ppermute | solution.py:233
  67.0 9.4 %copy-start.4 = (bf16[1040,128]{1,0:T(8,128)(2,1)}, bf16[1040,128]{1,0:T(8,128)(2,1)S(1)}, u32[]{:S(2)}) copy-start(bf16[1040,128]{1,0:T(8,128)(2,1)S(1)} %collective-permute-done.7.refs_4_) | copy-start | bytes 798724
  67.0 9.4 %collective-permute-start.8 = (bf16[1040,128]{1,0:T(8,128)(2,1)S(1)}, bf16[1040,128]{1,0:T(8,128)(2,1)S(1)}, u32[]{:S(2)}, u32[]{:S(2)}) collective-permute-start(bf16[1040,128]{1,0:T(8,128)(2,1)S(1)} %collective-permute-done.7.refs_4_), channel_id=1, source_target_pairs={{0,1},{1,2},{2,3},{3,0},{4,5},{5,6},{6,7},{7,4},{8,9},{9,10},{10,1... | collective-permute-start | bytes 798728 | tf_op jit(solution)/shard_map/ppermute | solution.py:233
  67.0 9.4 %copy-start = (bf16[128,4096]{1,0:T(8,128)(2,1)}, bf16[128,4096]{1,0:T(8,128)(2,1)S(1)}, u32[]{:S(2)}) copy-start(bf16[128,4096]{1,0:T(8,128)(2,1)S(1)} %collective-permute-done.4.refs_1_) | copy-start | bytes 3145732
  76.3 0.7 copy-start.5
  77.0 1.0 %copy-start.1 = (bf16[128,4096]{1,0:T(8,128)(2,1)}, bf16[128,4096]{1,0:T(8,128)(2,1)S(1)}, u32[]{:S(2)}) copy-start(bf16[128,4096]{1,0:T(8,128)(2,1)S(1)} %collective-permute-done.3.refs_0_) | copy-start | bytes 3145732

commit v2 on v1

--- a/solution.py
+++ b/solution.py
@@ -8,12 +8,14 @@
 from jax.experimental.pallas import tpu as pltpu
 from jax.sharding import PartitionSpec as P
 
+
 QUERY_HEADS = 64
 KEY_VALUE_HEADS = 8
 HEAD_SIZE = 128
 GROUP = QUERY_HEADS // KEY_VALUE_HEADS
 WIDTH = GROUP * HEAD_SIZE
 SEGMENT_ROWS = 16
+PAIR = 2
 
 rope_theta = 1000000.0
 yarn_factor = 4.0
@@ -115,13 +117,9 @@
     )(queries, cosine, sine)
 
 
-def attend_kernel(
-    before, after, count, blocks, here_ref, *refs
-):
-    ready = refs[: (before > 0) + (after > 0)]
-    refs = refs[len(ready) :]
+def attend_kernel(count, blocks, here_ref, *refs):
     queries_ref, payloads = refs[0], refs[1 : 1 + blocks]
-    out_ref, bias_ref, keys_ref, values_ref, scores_ref = refs[1 + blocks :]
+    out_ref, bias_ref, keys_ref, values_ref = refs[-4:]
     step = pl.program_id(0)
     rows = queries_ref.shape[0]
     segment_row = 2 * count * rows
@@ -140,11 +138,7 @@
             visible = visible & (lane + ahead <= row)
             bias_ref[:, b * rows : (b + 1) * rows] = jnp.where(visible, 0.0, masked_score)
 
-    active = (step >= before) & (step < before + count)
-
-    @pl.when(active)
-    def _():
-        g = step - before
+    def attend_group(g):
         for b in range(blocks):
             first = pl.multiple_of(g * rows, rows)
             keys_ref[b * rows : (b + 1) * rows, :] = payloads[b][pl.ds(first, rows), :]
@@ -152,85 +146,93 @@
             values_ref[b * rows : (b + 1) * rows, :] = payloads[b][pl.ds(first, rows), :]
         keys = keys_ref[...]
         values = values_ref[...]
-        scale = 1.0 / math.sqrt(HEAD_SIZE)
-        for h in range(GROUP):
-            columns = slice(h * HEAD_SIZE, (h + 1) * HEAD_SIZE)
-            scores = lax.dot_general(
-                queries_ref[:, columns],
+        rate = math.log2(math.e) / math.sqrt(HEAD_SIZE)
+
+        def scored(i):
+            heads = [
+                queries_ref[:, h * HEAD_SIZE : (h + 1) * HEAD_SIZE]
+                for h in range(i * PAIR, (i + 1) * PAIR)
+            ]
+            return lax.dot_general(
+                jnp.concatenate(heads, axis=0),
                 keys,
                 (((1,), (1,)), ((), ())),
                 preferred_element_type=jnp.float32,
             )
-            scores = scores * scale + bias_ref[...]
+
+        def finish(i, rounded, totals):
+            summed = jnp.dot(rounded, values, preferred_element_type=jnp.float32)
+            result = (summed / totals).astype(jnp.bfloat16)
+            for h in range(PAIR):
+                columns = slice((i * PAIR + h) * HEAD_SIZE, (i * PAIR + h + 1) * HEAD_SIZE)
+                out_ref[:, columns] = result[h * rows : (h + 1) * rows]
+
+        following = scored(0)
+        waiting = None
+        for i in range(GROUP // PAIR):
+            scores = following
+            if i + 1 < GROUP // PAIR:
+                following = scored(i + 1)
+            if waiting is not None:
+                finish(*waiting)
+            scores = scores.reshape(PAIR, rows, -1) + bias_ref[...][None]
+            scores = scores.reshape(PAIR * rows, -1)
             best = jnp.max(scores, axis=1, keepdims=True)
-            weights = jnp.exp(scores - best)
+            weights = jnp.exp2((scores - best) * rate)
             totals = jnp.sum(weights, axis=1, keepdims=True)
-            summed = jnp.dot(
-                weights.astype(jnp.bfloat16), values, preferred_element_type=jnp.float32
-            )
-            out_ref[:, columns] = (summed / totals).astype(jnp.bfloat16)
-
-    if before:
-
-        @pl.when(step < before)
-        def _():
-            out_ref[...] = ready[0][...]
-
-    if after:
-
-        @pl.when(step >= before + count)
-        def _():
-            out_ref[...] = ready[-1][...]
-
-
-def attend(queries, payloads, here, ready_before=None, ready_after=None):
+            waiting = (i, weights.astype(jnp.bfloat16), totals)
+        finish(*waiting)
+
+    attend_group(step)
+
+
+def attend(queries, payloads, here, first, done_before=None):
     rows = queries.shape[0]
     count = queries.shape[1] // WIDTH
     blocks = len(payloads)
-    before = 0 if ready_before is None else ready_before.shape[1] // WIDTH
-    after = 0 if ready_after is None else ready_after.shape[1] // WIDTH
-    total = before + count + after
-    ready, ready_specs = [], []
-    if before:
-        ready.append(ready_before)
-        ready_specs.append(pl.BlockSpec((rows, WIDTH), lambda g, s: (0, jnp.minimum(g, before - 1))))
-    if after:
-        ready.append(ready_after)
-        ready_specs.append(
-            pl.BlockSpec((rows, WIDTH), lambda g, s: (0, jnp.maximum(g - before - count, 0)))
-        )
     keys = blocks * rows
+    so_far = [] if done_before is None else [done_before]
     return pl.pallas_call(
-        functools.partial(attend_kernel, before, after, count, blocks),
+        functools.partial(attend_kernel, count, blocks),
         grid_spec=pltpu.PrefetchScalarGridSpec(
             num_scalar_prefetch=1,
-            grid=(total,),
+            grid=(count,),
             in_specs=[
-                *ready_specs,
-                pl.BlockSpec((rows, WIDTH), lambda g, s: (0, jnp.clip(g - before, 0, count - 1))),
+                pl.BlockSpec((rows, WIDTH), lambda g, s: (0, g)),
                 *[pl.BlockSpec(p.shape, lambda g, s: (0, 0)) for p in payloads],
+                *[pl.BlockSpec(memory_space=pl.ANY) for _ in so_far],
             ],
-            out_specs=pl.BlockSpec((rows, WIDTH), lambda g, s: (0, g)),
+            out_specs=pl.BlockSpec((rows, WIDTH), lambda g, s: (0, first + g)),
             scratch_shapes=[
                 pltpu.VMEM((rows, keys), jnp.float32),
                 pltpu.VMEM((keys, HEAD_SIZE), jnp.bfloat16),
                 pltpu.VMEM((keys, HEAD_SIZE), jnp.bfloat16),
-                pltpu.VMEM((rows, keys), jnp.float32),
             ],
         ),
-        out_shape=jax.ShapeDtypeStruct((rows, total * WIDTH), jnp.bfloat16),
+        out_shape=jax.ShapeDtypeStruct((rows, KEY_VALUE_HEADS * WIDTH), jnp.bfloat16),
+        input_output_aliases={2 + blocks: 0} if so_far else {},
         name="attend",
         cost_estimate=pl.CostEstimate(
             flops=4 * rows * keys * count * WIDTH,
             bytes_accessed=4 * rows * count * WIDTH,
             transcendentals=rows * keys * count * GROUP,
         ),
-    )(here, *ready, queries, *payloads)
+    )(here, queries, *payloads, *so_far)
 
 
 def ring(block, axis):
     size = lax.axis_size(axis)
     return lax.ppermute(block, axis, [(i, (i + 1) % size) for i in range(size)])
+
+
+def ring_both(block):
+    sections, size = lax.axis_size("pipe"), lax.axis_size("seq")
+    route = [
+        (p * size + z, (p + 1) % sections * size + (z + 1) % size)
+        for p in range(sections)
+        for z in range(size)
+    ]
+    return lax.ppermute(block, ("pipe", "seq"), route)
 
 
 CHUNKS = (4, 4)
@@ -240,20 +242,20 @@
     cosine, sine = yarn_tables(positions[0], HEAD_SIZE)
     here = lax.axis_index("seq").astype(jnp.int32).reshape(1)
     size = lax.axis_size("seq")
-    stay, move = CHUNKS
-    pay_stay, pay_move = pack(
-        CHUNKS, projected_keys[0], projected_values[0], segments, cosine, sine
-    )
-    pay_move = ring(pay_move, "pipe")
-    stay_blocks, move_blocks = [pay_stay], [pay_move]
-    queries_stay = rotate(query_states[0], 0, stay, cosine, sine)
-    queries_move = ring(rotate(query_states[0], stay, move, cosine, sine), "pipe")
-    for _ in range(size - 1):
-        stay_blocks.append(ring(stay_blocks[-1], "seq"))
-    for _ in range(size - 1):
-        move_blocks.append(ring(move_blocks[-1], "seq"))
-    out_stay = ring(attend(queries_stay, stay_blocks, here), "pipe")
-    return attend(queries_move, move_blocks, here, ready_before=out_stay)[None]
+    packed = pack(CHUNKS, projected_keys[0], projected_values[0], segments, cosine, sine)
+    held = [[] for _ in CHUNKS]
+    for c, payload in enumerate(packed):
+        held[c].append(ring(payload, "pipe"))
+        held[c].append(ring_both(payload))
+        for _ in range(2, size):
+            held[c].append(ring(held[c][-1], "seq"))
+    result, first = None, 0
+    for c, count in enumerate(CHUNKS):
+        queries = rotate(query_states[0], first, count, cosine, sine)
+        queries = ring(queries, "pipe")
+        result = attend(queries, held[c], here, first, result)
+        first += count
+    return result[None]
 
 
 def solution(mesh):

time: 91.7 us -> 62.7 us (0.68)
  waiting for transfers between devices: 48.5 us -> 30.5 us
  Pallas kernels: 34.3 us -> 21.2 us
  starting transfers between devices: 4.45 us -> 6.11 us
    ppermute x9 -> x8, waiting for transfers between devices: 48.5 us -> 16.1 us  [ring(): return lax.ppermute(block, axis, [(i, (i + 1) % size) for i in range(size)])]
    ppermute x0 -> x2, waiting for transfers between devices: none -> 14.5 us  [ring_both(): return lax.ppermute(block, ('pipe', 'seq'), route)]
    pallas_call x2, Pallas kernels: 24.6 us -> 11.6 us  [attend(): pl.pallas_call(functools.partial(attend_kernel, count, blocks), grid_spec...]
    ppermute x0 -> x2, starting transfers between devices: none -> 2.84 us  [ring_both(): return lax.ppermute(block, ('pipe', 'seq'), route)]
    ppermute x9 -> x8, starting transfers between devices: 4.45 us -> 3.26 us  [ring(): return lax.ppermute(block, axis, [(i, (i + 1) % size) for i in range(size)])]
    unnamed x18 -> x14, local copies, waits for them, and re-layouts: 2.35 us -> 2.77 us
  transfers between devices with their start and end apart: 9 -> 10, of which waited for: 5 -> 6; matrix products, arithmetic and copies ran while one was open for 0% -> 0% of each run, Pallas kernels for 21% -> 19%
where the time goes in v2:
time: 62.7 us; the launch traced here: 62.3 us
  waiting for transfers between devices  30.5 us (49%)
  Pallas kernels  21.2 us (34%)
  starting transfers between devices  6.11 us (10%)
  local copies, waits for them, and re-layouts  2.77 us (4%)
  other arithmetic  1.64 us (3%)
    ppermute x8, waiting for transfers between devices, ring(): return lax.ppermute(block, axis, [(i, (i + 1) % size) for i in range(size)])  16.1 us
    ppermute x2, waiting for transfers between devices, ring_both(): return lax.ppermute(block, ('pipe', 'seq'), route)  14.5 us
    pallas_call x2, Pallas kernels, attend(): pl.pallas_call(functools.partial(attend_kernel, count, blocks), grid_spec...  11.6 us
    pallas_call x2, Pallas kernels, rotate(): pl.pallas_call(rotate_kernel, grid=(count,), in_specs=[pl.BlockSpec((rows...  7.51 us
    ppermute x8, starting transfers between devices, ring(): return lax.ppermute(block, axis, [(i, (i + 1) % size) for i in range(size)])  3.26 us
    ppermute x2, starting transfers between devices, ring_both(): return lax.ppermute(block, ('pipe', 'seq'), route)  2.84 us
    unnamed x14, local copies, waits for them, and re-layouts  2.77 us
    pallas_call x1, Pallas kernels, pack(): pl.pallas_call(functools.partial(pack_kernel, groups), out_shape=[jax.Sha...  2.05 us
  transfers between devices with their start and end apart: 10, of which 6 were waited for; matrix products, arithmetic and copies ran while one was open for 0% of the time, Pallas kernels for 19%

profile of v2, /device:TPU:0, one launch (start us, length us, event | category | flops | bytes accessed | tf_op | source)
XLA Modules:
  0.0 62.3 jit_solution(15824274108140442609)
XLA Ops:
  0.0 0.7 %convert_bitcast_fusion = f32[128]{0:T(128)S(1)} fusion(s32[1,128]{1,0:T(1,128)} %param.8), kind=kLoop, calls=%fused_computation.12 | loop fusion | flops 128 | bytes 1024 | tf_op jit(solution)/shard_map/convert_element_type | solution.py:49
  0.7 1.0 %fusion.1 = (f32[128,64]{1,0:T(8,128)}, f32[128,64]{1,0:T(8,128)}) fusion(f32[64]{0:T(128)S(1)} %multiply_add_fusion, f32[128]{0:T(128)S(1)} %convert_bitcast_fusion), kind=kLoop, calls=%fused_computation.3 | loop fusion | flops 24576 | bytes 66304 | tf_op jit(solution)/shard_map/mul | solution.py:50
  1.6 3.8 %rotate.3 = bf16[128,4096]{1,0:T(8,128)(2,1)} custom-call(bf16[128,8192]{1,0:T(8,128)(2,1)} %bitcast.7, f32[128,64]{1,0:T(8,128)} %get-tuple-element.10.cos_ref, f32[128,64]{1,0:T(8,128)} %get-tuple-element.9.sin_ref), custom_call_target="tpu_custom_call" | custom-call | flops 2097152 | bytes 2097152 | tf_op jit(solution)/shard_map/rotate/pallas_call | solution.py:101
  5.4 0.5 collective-permute-start.5
  5.9 3.8 %rotate.2 = bf16[128,4096]{1,0:T(8,128)(2,1)} custom-call(bf16[128,8192]{1,0:T(8,128)(2,1)} %bitcast.8, f32[128,64]{1,0:T(8,128)} %get-tuple-element.10.cos_ref, f32[128,64]{1,0:T(8,128)} %get-tuple-element.9.sin_ref), custom_call_target="tpu_custom_call" | custom-call | flops 2097152 | bytes 2097152 | tf_op jit(solution)/shard_map/rotate/pallas_call | solution.py:101
  9.6 2.6 %collective-permute-start = (bf16[128,4096]{1,0:T(8,128)(2,1)}, bf16[128,4096]{1,0:T(8,128)(2,1)S(1)}, u32[]{:S(2)}, u32[]{:S(2)}) collective-permute-start(bf16[128,4096]{1,0:T(8,128)(2,1)} %rotate.2), channel_id=1, source_target_pairs={{0,4},{4,8},{8,12},{12,0},{1,5},{5,9},{9,13},{13,1},{2,6},{6,10},{... | collective-permute-start | bytes 3145736 | tf_op jit(solution)/shard_map/ppermute | solution.py:225
  12.2 2.1 %pack.1 = (bf16[1040,128]{1,0:T(8,128)(2,1)}, bf16[1040,128]{1,0:T(8,128)(2,1)}) custom-call(bf16[128,1024]{1,0:T(8,128)(2,1)} %bitcast.9, bf16[128,1024]{1,0:T(8,128)(2,1)} %bitcast.10, s32[1,128]{1,0:T(1,128)} %segment_ref.1, f32[128,64]{1,0:T(8,128)} %get-tuple-element.10.cos_ref, f32[128,64]{1,0:T(8,128)} %get-tuple-element.9.sin_ref), custom_call_target="tpu_custom_call" | custom-call | flops 1048576 | bytes 1048576 | tf_op jit(solution)/shard_map/pack/pallas_call | solution.py:79
  14.3 1.2 %collective-permute-start.7 = (bf16[1040,128]{1,0:T(8,128)(2,1)}, bf16[1040,128]{1,0:T(8,128)(2,1)S(1)}, u32[]{:S(2)}, u32[]{:S(2)}) collective-permute-start(bf16[1040,128]{1,0:T(8,128)(2,1)} %get-tuple-element.8), channel_id=1, source_target_pairs={{0,5},{1,6},{2,7},{3,4},{4,9},{5,10},{6,11},{7,8},{8,13},{9,14},{1... | collective-permute-start | bytes 798728 | tf_op jit(solution)/shard_map/ppermute | solution.py:235
  15.5 1.6 %collective-permute-start.2 = (bf16[1040,128]{1,0:T(8,128)(2,1)}, bf16[1040,128]{1,0:T(8,128)(2,1)S(1)}, u32[]{:S(2)}, u32[]{:S(2)}) collective-permute-start(bf16[1040,128]{1,0:T(8,128)(2,1)} %get-tuple-element.7), channel_id=1, source_target_pairs={{0,5},{1,6},{2,7},{3,4},{4,9},{5,10},{6,11},{7,8},{8,13},{9,14},{1... | collective-permute-start | bytes 798728 | tf_op jit(solution)/shard_map/ppermute | solution.py:235
  17.1 8.8 %collective-permute-done.7.refs_2_ = bf16[1040,128]{1,0:T(8,128)(2,1)S(1)} collective-permute-done((bf16[1040,128]{1,0:T(8,128)(2,1)}, bf16[1040,128]{1,0:T(8,128)(2,1)S(1)}, u32[]{:S(2)}, u32[]{:S(2)}) %collective-permute-start.7) | collective-permute-done | bytes 266272 | tf_op jit(solution)/shard_map/ppermute | solution.py:235
  25.9 0.0 collective-permute-start.8
  25.9 0.0 collective-permute-start.6
  25.9 5.7 %collective-permute-done.2.refs_2_ = bf16[1040,128]{1,0:T(8,128)(2,1)S(1)} collective-permute-done((bf16[1040,128]{1,0:T(8,128)(2,1)}, bf16[1040,128]{1,0:T(8,128)(2,1)S(1)}, u32[]{:S(2)}, u32[]{:S(2)}) %collective-permute-start.2) | collective-permute-done | bytes 266272 | tf_op jit(solution)/shard_map/ppermute | solution.py:235
  31.6 0.0 collective-permute-start.3
  31.6 5.3 %collective-permute-done.8.refs_3_ = bf16[1040,128]{1,0:T(8,128)(2,1)} collective-permute-done((bf16[1040,128]{1,0:T(8,128)(2,1)S(1)}, bf16[1040,128]{1,0:T(8,128)(2,1)}, u32[]{:S(2)}, u32[]{:S(2)}) %collective-permute-start.8) | collective-permute-done | bytes 266272 | tf_op jit(solution)/shard_map/ppermute | solution.py:225
  36.9 0.0 collective-permute-start.9
  36.9 3.5 %collective-permute-done.6.refs_1_ = bf16[1040,128]{1,0:T(8,128)(2,1)} collective-permute-done((bf16[1040,128]{1,0:T(8,128)(2,1)}, bf16[1040,128]{1,0:T(8,128)(2,1)}, u32[]{:S(2)}, u32[]{:S(2)}) %collective-permute-start.6) | collective-permute-done | bytes 266272 | tf_op jit(solution)/shard_map/ppermute | solution.py:225
  40.4 0.0 collective-permute-start.1
  40.4 2.3 %collective-permute-done.3.refs_3_ = bf16[1040,128]{1,0:T(8,128)(2,1)S(1)} collective-permute-done((bf16[1040,128]{1,0:T(8,128)(2,1)S(1)}, bf16[1040,128]{1,0:T(8,128)(2,1)S(1)}, u32[]{:S(2)}, u32[]{:S(2)}) %collective-permute-start.3) | collective-permute-done | bytes 266272 | tf_op jit(solution)/shard_map/ppermute | solution.py:225
  42.7 0.2 collective-permute-start.4
  42.8 5.0 %collective-permute-done.9.refs_4_ = bf16[1040,128]{1,0:T(8,128)(2,1)} collective-permute-done((bf16[1040,128]{1,0:T(8,128)(2,1)}, bf16[1040,128]{1,0:T(8,128)(2,1)}, u32[]{:S(2)}, u32[]{:S(2)}) %collective-permute-start.9) | collective-permute-done | bytes 266272 | tf_op jit(solution)/shard_map/ppermute | solution.py:225
  47.8 0.0 collective-permute-done.5.refs_0_
  47.8 0.0 copy-done.6
  47.8 1.0 %copy-done.1 = bf16[128,4096]{1,0:T(8,128)(2,1)} copy-done((bf16[128,4096]{1,0:T(8,128)(2,1)}, bf16[128,4096]{1,0:T(8,128)(2,1)S(1)}, u32[]{:S(2)}) %copy-start.1) | copy-done | bytes 1048600
  48.8 5.8 %attend.2.refs_5_ = bf16[128,8192]{1,0:T(8,128)(2,1)} custom-call(s32[1]{0:T(128)} %bitcast.here_ref, bf16[128,4096]{1,0:T(8,128)(2,1)} %copy-done.1, bf16[1040,128]{1,0:T(8,128)(2,1)} %collective-permute-done.6.refs_1_, bf16[1040,128]{1,0:T(8,128)(2,1)} %copy-done.6, bf16[1040,128]{1,0:T(8,128)(2,1)} %collective-permute-done.8.refs_3_, ...), custom_call_target="tpu_custom_call" | custom-call | flops 1073741824 | bytes 2097152 | tf_op jit(solution)/shard_map/attend/pallas_call | solution.py:195
  54.6 0.0 collective-permute-done.1.refs_1_
  54.6 0.0 collective-permute-done.4.refs_4_
  54.7 0.0 collective-permute-done.refs_0_
  54.7 0.7 %copy-done.4 = bf16[1040,128]{1,0:T(8,128)(2,1)} copy-done((bf16[1040,128]{1,0:T(8,128)(2,1)}, bf16[1040,128]{1,0:T(8,128)(2,1)S(1)}, u32[]{:S(2)}) %copy-start.4) | copy-done | bytes 266264
  55.3 0.1 copy-done.5
  55.5 1.0 %copy-done = bf16[128,4096]{1,0:T(8,128)(2,1)} copy-done((bf16[128,4096]{1,0:T(8,128)(2,1)}, bf16[128,4096]{1,0:T(8,128)(2,1)S(1)}, u32[]{:S(2)}) %copy-start) | copy-done | bytes 1048600
  56.5 5.8 %attend.3 = bf16[128,8192]{1,0:T(8,128)(2,1)} custom-call(s32[1]{0:T(128)} %bitcast.here_ref, bf16[128,4096]{1,0:T(8,128)(2,1)} %copy-done, bf16[1040,128]{1,0:T(8,128)(2,1)} %copy-done.4, bf16[1040,128]{1,0:T(8,128)(2,1)} %copy-done.2, bf16[1040,128]{1,0:T(8,128)(2,1)} %copy-done.3, bf16[1040,128]{1,0:T(8,128)(2,1)} %copy-done.5, ...), custom_call_target="tpu_custom_call", output_to_operand_aliasing={{}: (6, {})} | custom-call | flops 1073741824 | bytes 2097152 | tf_op jit(solution)/shard_map/attend/pallas_call | solution.py:195
  (10 shorter events, 0.0 us)
Async XLA Ops:
  5.4 42.4 %collective-permute-start.5 = (bf16[128,4096]{1,0:T(8,128)(2,1)}, bf16[128,4096]{1,0:T(8,128)(2,1)S(1)}, u32[]{:S(2)}, u32[]{:S(2)}) collective-permute-start(bf16[128,4096]{1,0:T(8,128)(2,1)} %rotate.3), channel_id=1, source_target_pairs={{0,4},{4,8},{8,12},{12,0},{1,5},{5,9},{9,13},{13,1},{2,6},{6,10},{... | collective-permute-start | bytes 3145736 | tf_op jit(solution)/shard_map/ppermute | solution.py:225
  9.6 45.0 %collective-permute-start = (bf16[128,4096]{1,0:T(8,128)(2,1)}, bf16[128,4096]{1,0:T(8,128)(2,1)S(1)}, u32[]{:S(2)}, u32[]{:S(2)}) collective-permute-start(bf16[128,4096]{1,0:T(8,128)(2,1)} %rotate.2), channel_id=1, source_target_pairs={{0,4},{4,8},{8,12},{12,0},{1,5},{5,9},{9,13},{13,1},{2,6},{6,10},{... | collective-permute-start | bytes 3145736 | tf_op jit(solution)/shard_map/ppermute | solution.py:225
  14.3 11.6 %collective-permute-start.7 = (bf16[1040,128]{1,0:T(8,128)(2,1)}, bf16[1040,128]{1,0:T(8,128)(2,1)S(1)}, u32[]{:S(2)}, u32[]{:S(2)}) collective-permute-start(bf16[1040,128]{1,0:T(8,128)(2,1)} %get-tuple-element.8), channel_id=1, source_target_pairs={{0,5},{1,6},{2,7},{3,4},{4,9},{5,10},{6,11},{7,8},{8,13},{9,14},{1... | collective-permute-start | bytes 798728 | tf_op jit(solution)/shard_map/ppermute | solution.py:235
  15.5 16.1 %collective-permute-start.2 = (bf16[1040,128]{1,0:T(8,128)(2,1)}, bf16[1040,128]{1,0:T(8,128)(2,1)S(1)}, u32[]{:S(2)}, u32[]{:S(2)}) collective-permute-start(bf16[1040,128]{1,0:T(8,128)(2,1)} %get-tuple-element.7), channel_id=1, source_target_pairs={{0,5},{1,6},{2,7},{3,4},{4,9},{5,10},{6,11},{7,8},{8,13},{9,14},{1... | collective-permute-start | bytes 798728 | tf_op jit(solution)/shard_map/ppermute | solution.py:235
  25.9 21.9 %copy-start.6 = (bf16[1040,128]{1,0:T(8,128)(2,1)}, bf16[1040,128]{1,0:T(8,128)(2,1)S(1)}, u32[]{:S(2)}) copy-start(bf16[1040,128]{1,0:T(8,128)(2,1)S(1)} %collective-permute-done.7.refs_2_) | copy-start | bytes 798724
  25.9 11.0 %collective-permute-start.8 = (bf16[1040,128]{1,0:T(8,128)(2,1)S(1)}, bf16[1040,128]{1,0:T(8,128)(2,1)}, u32[]{:S(2)}, u32[]{:S(2)}) collective-permute-start(bf16[1040,128]{1,0:T(8,128)(2,1)S(1)} %collective-permute-done.7.refs_2_), channel_id=1, source_target_pairs={{0,1},{1,2},{2,3},{3,0},{4,5},{5,6},{6,7},{7,4},{8,9},{9,10},{10,1... | collective-permute-start | bytes 798728 | tf_op jit(solution)/shard_map/ppermute | solution.py:225
  25.9 14.5 %collective-permute-start.6 = (bf16[1040,128]{1,0:T(8,128)(2,1)}, bf16[1040,128]{1,0:T(8,128)(2,1)}, u32[]{:S(2)}, u32[]{:S(2)}) collective-permute-start(bf16[1040,128]{1,0:T(8,128)(2,1)} %get-tuple-element.8), channel_id=1, source_target_pairs={{0,4},{4,8},{8,12},{12,0},{1,5},{5,9},{9,13},{13,1},{2,6},{6,10},{... | collective-permute-start | bytes 798728 | tf_op jit(solution)/shard_map/ppermute | solution.py:225
  31.6 23.1 %copy-start.2 = (bf16[1040,128]{1,0:T(8,128)(2,1)}, bf16[1040,128]{1,0:T(8,128)(2,1)S(1)}, u32[]{:S(2)}) copy-start(bf16[1040,128]{1,0:T(8,128)(2,1)S(1)} %collective-permute-done.2.refs_2_) | copy-start | bytes 798724
  31.6 11.1 %collective-permute-start.3 = (bf16[1040,128]{1,0:T(8,128)(2,1)S(1)}, bf16[1040,128]{1,0:T(8,128)(2,1)S(1)}, u32[]{:S(2)}, u32[]{:S(2)}) collective-permute-start(bf16[1040,128]{1,0:T(8,128)(2,1)S(1)} %collective-permute-done.2.refs_2_), channel_id=1, source_target_pairs={{0,1},{1,2},{2,3},{3,0},{4,5},{5,6},{6,7},{7,4},{8,9},{9,10},{10,1... | collective-permute-start | bytes 798728 | tf_op jit(solution)/shard_map/ppermute | solution.py:225
  36.9 11.0 %collective-permute-start.9 = (bf16[1040,128]{1,0:T(8,128)(2,1)}, bf16[1040,128]{1,0:T(8,128)(2,1)}, u32[]{:S(2)}, u32[]{:S(2)}) collective-permute-start(bf16[1040,128]{1,0:T(8,128)(2,1)} %collective-permute-done.8.refs_3_), channel_id=1, source_target_pairs={{0,1},{1,2},{2,3},{3,0},{4,5},{5,6},{6,7},{7,4},{8,9},{9,10},{10,1... | collective-permute-start | bytes 798728 | tf_op jit(solution)/shard_map/ppermute | solution.py:225
  40.4 14.2 %collective-permute-start.1 = (bf16[1040,128]{1,0:T(8,128)(2,1)}, bf16[1040,128]{1,0:T(8,128)(2,1)S(1)}, u32[]{:S(2)}, u32[]{:S(2)}) collective-permute-start(bf16[1040,128]{1,0:T(8,128)(2,1)} %get-tuple-element.7), channel_id=1, source_target_pairs={{0,4},{4,8},{8,12},{12,0},{1,5},{5,9},{9,13},{13,1},{2,6},{6,10},{... | collective-permute-start | bytes 798728 | tf_op jit(solution)/shard_map/ppermute | solution.py:225
  42.7 12.0 %copy-start.3 = (bf16[1040,128]{1,0:T(8,128)(2,1)}, bf16[1040,128]{1,0:T(8,128)(2,1)S(1)}, u32[]{:S(2)}) copy-start(bf16[1040,128]{1,0:T(8,128)(2,1)S(1)} %collective-permute-done.3.refs_3_) | copy-start | bytes 798724
  42.7 12.0 %collective-permute-start.4 = (bf16[1040,128]{1,0:T(8,128)(2,1)S(1)}, bf16[1040,128]{1,0:T(8,128)(2,1)S(1)}, u32[]{:S(2)}, u32[]{:S(2)}) collective-permute-start(bf16[1040,128]{1,0:T(8,128)(2,1)S(1)} %collective-permute-done.3.refs_3_), channel_id=1, source_target_pairs={{0,1},{1,2},{2,3},{3,0},{4,5},{5,6},{6,7},{7,4},{8,9},{9,10},{10,1... | collective-permute-start | bytes 798728 | tf_op jit(solution)/shard_map/ppermute | solution.py:225
  47.8 1.0 %copy-start.1 = (bf16[128,4096]{1,0:T(8,128)(2,1)}, bf16[128,4096]{1,0:T(8,128)(2,1)S(1)}, u32[]{:S(2)}) copy-start(bf16[128,4096]{1,0:T(8,128)(2,1)S(1)} %collective-permute-done.5.refs_0_) | copy-start | bytes 3145732
  54.6 0.7 %copy-start.4 = (bf16[1040,128]{1,0:T(8,128)(2,1)}, bf16[1040,128]{1,0:T(8,128)(2,1)S(1)}, u32[]{:S(2)}) copy-start(bf16[1040,128]{1,0:T(8,128)(2,1)S(1)} %collective-permute-done.1.refs_1_) | copy-start | bytes 798724
  54.7 0.8 %copy-start.5 = (bf16[1040,128]{1,0:T(8,128)(2,1)}, bf16[1040,128]{1,0:T(8,128)(2,1)S(1)}, u32[]{:S(2)}) copy-start(bf16[1040,128]{1,0:T(8,128)(2,1)S(1)} %collective-permute-done.4.refs_4_) | copy-start | bytes 798724
  55.5 1.0 %copy-start = (bf16[128,4096]{1,0:T(8,128)(2,1)}, bf16[128,4096]{1,0:T(8,128)(2,1)S(1)}, u32[]{:S(2)}) copy-start(bf16[128,4096]{1,0:T(8,128)(2,1)S(1)} %collective-permute-done.refs_0_) | copy-start | bytes 3145732
